TPU v7x, 256 devices: a whole 4x4x8 slice. The times are simulated.
256 devices in a mesh: dp: 64 (over x, z_hi, y), section: 4 (over z_lo, core).
Axes of the slice: x: 4, y: 4, z: 8 (z_hi: 4, z_lo: 2; z = z_hi * 2 + z_lo), core: 2. Of those that a mesh axis runs over, the one named last changes fastest.
Arguments:
- inputs: bfloat16 [2, 4096, 1024], P(None, 'dp'), may hold values from -6 to 6
- ln_gain: float32 [4, 1024], P('section'), may hold values from 0.5 to 1.5
- w_in: bfloat16 [4, 1024, 2048], P('section'), may hold values from -0.1875 to 0.1875
- w_out: bfloat16 [4, 2048, 1024], P('section'), may hold values from -0.125 to 0.125
- layer_scale: float32 [4, 1024], P('section'), may hold values from 0.25 to 1
- out_grad: bfloat16 [2, 4096, 1024], P(None, 'dp'), may hold values from -6 to 6
- owner_table: int32 [64], replicated, may hold values from 0 to 63, each once
Outputs:
- act_factor: float32 [4, 1024, 1024], P('section', 'dp')
- grad_factor: float32 [4, 2048, 2048], P('section', 'dp')
Inputs may be any that keep to these rules, and one draw needn't show every extreme that they name: owner_table holds each of 0 .. 63 once.
All inputs are finite; a program needn't handle non-finite values.
Results may differ from a plain program's by a relative error of at most 0.009.
Values may be sent and summed in bfloat16 or wider, within the bound.
A program may use at most 128 MiB of HBM per device.

v0:
```python
import jax
import jax.numpy as jnp
from jax import lax
from jax.sharding import PartitionSpec as P

SQRT_HALF = 0.7071067811865476
INV_ROOT_TAU = 0.3989422804014327


def passed_along(value, axis, steps):
    count = lax.axis_size(axis)
    initial, last = (max(0, -steps), min(count, count - steps))
    return lax.ppermute(value, axis, [(source, source + steps) for source in range(initial, last)])


def gelu_exact(values):
    return 0.5 * values * (1.0 + jax.scipy.special.erf(values * SQRT_HALF))


def gelu_slope(values):
    return 0.5 * (
        1.0 + jax.scipy.special.erf(values * SQRT_HALF)
    ) + values * INV_ROOT_TAU * jnp.exp(-0.5 * values * values)


def normalize(activations, gain_row):
    floats = activations.astype(jnp.float32)
    center = floats - jnp.mean(floats, axis=-1, keepdims=True)
    inv_std = lax.rsqrt(jnp.mean(center * center, axis=-1, keepdims=True) + 1e-06)
    normed = center * inv_std
    return ((normed * gain_row).astype(jnp.bfloat16), normed, inv_std)


def forward_block(activations, gain_row, weight_in, weight_out, scales):
    normed_bf, normed, inv_std = normalize(activations, gain_row)
    hidden = jnp.dot(normed_bf, weight_in, preferred_element_type=jnp.float32)
    activated = gelu_exact(hidden).astype(jnp.bfloat16)
    branch = jnp.dot(activated, weight_out, preferred_element_type=jnp.float32)
    output = (activations.astype(jnp.float32) + scales * branch).astype(jnp.bfloat16)
    return (output, normed_bf, normed, inv_std, hidden)


def backward_block(cotangent, normed, inv_std, hidden, gain_row, weight_in, weight_out, scales):
    scaled = (cotangent.astype(jnp.float32) * scales).astype(jnp.bfloat16)
    grad_act = lax.dot_general(
        scaled, weight_out, (((1,), (1,)), ((), ())), preferred_element_type=jnp.float32
    )
    grad_hidden = (grad_act * gelu_slope(hidden)).astype(jnp.bfloat16)
    grad_normed = (
        lax.dot_general(
            grad_hidden, weight_in, (((1,), (1,)), ((), ())), preferred_element_type=jnp.float32
        )
        * gain_row
    )
    mean_one = jnp.mean(grad_normed, axis=-1, keepdims=True)
    mean_two = jnp.mean(grad_normed * normed, axis=-1, keepdims=True)
    grad_input = cotangent.astype(jnp.float32) + inv_std * (
        grad_normed - mean_one - normed * mean_two
    )
    return (grad_input.astype(jnp.bfloat16), grad_hidden)


def block_columns(data, owner_table):
    owners = owner_table.shape[0]
    row_total, col_total = data.shape
    split = data.reshape(row_total, owners, col_total // owners)
    return jnp.take(split, owner_table, axis=1).reshape(row_total, col_total)


def square_term(permuted, plain, total_rows):
    product = lax.dot_general(
        permuted, plain, (((0,), (0,)), ((), ())), preferred_element_type=jnp.float32
    )
    return product / total_rows


def slot_of(position, batch_count):
    valid = (position >= 0) & (position < batch_count)
    return jnp.where(valid, position, batch_count)


def body(inputs, ln_gain, w_in, w_out, layer_scale, out_grad, owner_table):
    gain_row = ln_gain[0]
    weight_in = w_in[0]
    weight_out = w_out[0]
    scales = layer_scale[0]
    section_count = lax.axis_size("section")
    dp_count = lax.axis_size("dp")
    section_index = lax.axis_index("section")
    batch_count, row_count, width_in = inputs.shape
    width_hidden = weight_in.shape[1]
    total_rows = batch_count * row_count * dp_count
    tick_count = batch_count + section_count - 1
    saved_bf = jnp.zeros((batch_count + 1, row_count, width_in), jnp.bfloat16)
    saved_normed = jnp.zeros((batch_count + 1, row_count, width_in), jnp.float32)
    saved_inv = jnp.zeros((batch_count + 1, row_count, 1), jnp.float32)
    saved_hidden = jnp.zeros((batch_count + 1, row_count, width_hidden), jnp.float32)
    arriving = jnp.zeros((row_count, width_in), jnp.bfloat16)
    for tick_step in range(tick_count):
        first_input = inputs[min(tick_step, batch_count - 1)]
        incoming = jnp.where(section_index == 0, first_input, arriving)
        output, normed_bf, normed, inv_std, hidden = forward_block(
            incoming, gain_row, weight_in, weight_out, scales
        )
        slot_index = slot_of(tick_step - section_index, batch_count)
        saved_bf = lax.dynamic_update_index_in_dim(saved_bf, normed_bf, slot_index, 0)
        saved_normed = lax.dynamic_update_index_in_dim(saved_normed, normed, slot_index, 0)
        saved_inv = lax.dynamic_update_index_in_dim(saved_inv, inv_std, slot_index, 0)
        saved_hidden = lax.dynamic_update_index_in_dim(saved_hidden, hidden, slot_index, 0)
        if tick_step + 1 < tick_count:
            arriving = passed_along(output, "section", 1)
    grad_saved = jnp.zeros((batch_count + 1, row_count, width_hidden), jnp.bfloat16)
    returning = jnp.zeros((row_count, width_in), jnp.bfloat16)
    for tick_step in range(tick_count):
        position = tick_step - (section_count - 1 - section_index)
        pick_index = jnp.clip(position, 0, batch_count - 1)
        top_grad = out_grad[min(tick_step, batch_count - 1)]
        cotangent = jnp.where(section_index == section_count - 1, top_grad, returning)
        normed = lax.dynamic_index_in_dim(saved_normed, pick_index, 0, keepdims=False)
        inv_std = lax.dynamic_index_in_dim(saved_inv, pick_index, 0, keepdims=False)
        hidden = lax.dynamic_index_in_dim(saved_hidden, pick_index, 0, keepdims=False)
        grad_input, grad_hidden = backward_block(
            cotangent, normed, inv_std, hidden, gain_row, weight_in, weight_out, scales
        )
        grad_saved = lax.dynamic_update_index_in_dim(
            grad_saved, grad_hidden, slot_of(position, batch_count), 0
        )
        if tick_step + 1 < tick_count:
            returning = passed_along(grad_input, "section", -1)
    act_rows = saved_bf[:batch_count].reshape(batch_count * row_count, width_in)
    grad_rows = grad_saved[:batch_count].reshape(batch_count * row_count, width_hidden)
    act_perm = block_columns(act_rows, owner_table)
    grad_perm = block_columns(grad_rows, owner_table)
    act_share = lax.psum_scatter(
        square_term(act_perm, act_rows, total_rows), "dp", scatter_dimension=0, tiled=True
    )
    grad_share = lax.psum_scatter(
        square_term(grad_perm, grad_rows, total_rows), "dp", scatter_dimension=0, tiled=True
    )
    return (act_share[None], grad_share[None])


def solution(mesh):
    placed = (
        P(None, "dp", None),
        P("section", None),
        P("section", None, None),
        P("section", None, None),
        P("section", None),
        P(None, "dp", None),
        P(),
    )
    return jax.shard_map(
        body,
        mesh=mesh,
        in_specs=placed,
        out_specs=(P("section", "dp", None), P("section", "dp", None)),
        check_vma=False,
    )
```

profile of v0, /device:TPU:8, one launch (start us, length us, event | category | flops | bytes accessed | tf_op | source)
XLA Modules:
  0.0 889.6 jit_solution(11268334105578307453)
XLA Ops:
  9.6 3.3 bitcast_dynamic-update-slice_fusion.3
  13.9 1.7 collective-permute-start
  17.3 3.4 bitcast_dynamic-update-slice_fusion.2
  21.6 4.7 collective-permute-start.1
  29.7 5.3 collective-permute-start.2
  38.1 5.3 collective-permute-start.3
  48.1 2.6 convolution_multiply_fusion.1
  51.7 3.5 fusion.54
  57.4 1.5 fusion.263
  59.7 1.5 collective-permute-start.4
  61.2 4.9 collective-permute-done.4
  66.0 3.6 bitcast_dynamic-update-slice_fusion.6
  69.6 1.5 fusion.262
  73.3 6.3 collective-permute-done.5
  79.6 3.6 bitcast_dynamic-update-slice_fusion.5
  83.2 1.5 fusion.261
  86.8 5.6 collective-permute-done.6
  92.4 3.6 bitcast_dynamic-update-slice_fusion.4
  96.0 1.5 fusion.260
  99.6 5.2 collective-permute-done.7
  104.8 3.6 fusion.75
  110.5 8.0 convolution_multiply_fusion
  118.6 327.0 %reduce-scatter.3.cloned.1.call-done = f32[16,1024]{1,0:T(8,128)} async-done(((f32[1024,1024]{1,0:T(8,128)}), f32[16,1024]{1,0:T(8,128)}) %reduce-scatter.3.cloned.1.call-update) | async-done | bytes 65552 | tf_op jit(solution)/shard_map/reduce_scatter | solution.py:134
  445.5 437.2 %reduce-scatter.5.cloned.1.call-done = f32[32,2048]{1,0:T(8,128)} async-done(((f32[2048,2048]{1,0:T(8,128)}), f32[32,2048]{1,0:T(8,128)}) %reduce-scatter.5.cloned.1.call-update) | async-done | bytes 262160 | tf_op jit(solution)/shard_map/reduce_scatter | solution.py:137
  (119 shorter events, 28.9 us)
Async XLA Ops:
  7.2 5.8 copy-start.8
  7.2 5.8 copy-start.11
  7.2 438.4 %reduce-scatter.3.cloned.1.call-start = ((), (), s32[]{:S(2)}) async-start(), calls=%async_computation.2 | async-start | bytes 4259840 | tf_op jit(solution)/shard_map/reduce_scatter | solution.py:134
  9.6 6.0 copy-start.17
  9.6 6.7 copy-start.10
  13.9 2.8 collective-permute-start
  20.7 7.2 copy-start
  21.6 5.7 collective-permute-start.1
  29.7 6.3 collective-permute-start.2
  38.1 9.8 %copy-start.12 = (pred[64]{0:T(512)(128)(4,1)S(1)}, pred[64]{0:T(512)(128)(4,1)}, u32[]{:S(2)}) copy-start(pred[64]{0:T(512)(128)(4,1)} %compare_and_fusion) | copy-start | bytes 196
  38.1 6.3 collective-permute-start.3
  50.8 4.5 copy-start.9
  50.8 832.0 %reduce-scatter.5.cloned.1.call-start = ((), (), s32[]{:S(2)}) async-start(), calls=%async_computation.3 | async-start | bytes 17039360 | tf_op jit(solution)/shard_map/reduce_scatter | solution.py:137
  50.8 4.5 copy-start.7
  59.7 6.3 collective-permute-start.4
  61.2 8.5 copy-start.2
  66.0 5.1 copy-start.16
  72.0 7.6 collective-permute-start.5
  73.3 9.9 %copy-start.3 = (bf16[1,1024,2048]{2,1,0:T(8,128)(2,1)S(1)}, bf16[1,1024,2048]{2,1,0:T(8,128)(2,1)}, u32[]{:S(2)}) copy-start(bf16[1,1024,2048]{2,1,0:T(8,128)(2,1)} %param.9) | copy-start | bytes 12582916
  79.6 5.1 copy-start.15
  85.5 6.9 collective-permute-start.6
  86.8 9.2 %copy-start.4 = (bf16[1,1024,2048]{2,1,0:T(8,128)(2,1)S(1)}, bf16[1,1024,2048]{2,1,0:T(8,128)(2,1)}, u32[]{:S(2)}) copy-start(bf16[1,1024,2048]{2,1,0:T(8,128)(2,1)} %param.9) | copy-start | bytes 12582916
  92.4 5.1 copy-start.14
  98.3 6.5 collective-permute-start.7
  (4 other events, 11.8 us)
Sparse Core Ops, SparseCore 0:
  50.9 394.6 reduce-scatter.2
  448.7 434.0 reduce-scatter.4
where the time goes:
time: 896 us; the launch traced here: 890 us
  waiting for transfers between devices  789 us (88%)
  matrix products  48 us (5%)
  starting transfers between devices  22.5 us (3%)
  between operations  14.8 us (2%)
    reduce_scatter x1, waiting for transfers between devices, body(): lax.psum_scatter(square_term(grad_perm, grad_rows, total_rows), 'dp', sca...  437 us
    reduce_scatter x1, waiting for transfers between devices, body(): lax.psum_scatter(square_term(act_perm, act_rows, total_rows), 'dp', scatt...  327 us
    ppermute x8, waiting for transfers between devices, passed_along(): lax.ppermute(value, axis, [(source, source + steps) for source in range(i...  24.6 us
    ppermute x8, starting transfers between devices, passed_along(): lax.ppermute(value, axis, [(source, source + steps) for source in range(i...  22.4 us
  transfers between devices with their start and end apart: 10, of which 9 were waited for; matrix products, arithmetic and copies ran while one was open for 5% of the time, Pallas kernels for 0%

commit v1 on v0

v1 whole, which is shorter than its diff:
```python
import functools
import jax
import jax.numpy as jnp
from jax import lax
from jax.experimental import pallas as pl
from jax.experimental.pallas import tpu as pltpu
from jax.sharding import PartitionSpec as P

SQRT_HALF = 0.7071067811865476
INV_ROOT_TAU = 0.3989422804014327
MESH = pl.DeviceIdType.MESH
F32 = jnp.float32
BF16 = jnp.bfloat16
NT = (((1,), (1,)), ((), ()))


def cube_side(count):
    side = 1
    while side**3 < count:
        side += 1
    return side


def kernel(
    dp_count,
    sections,
    owner_ref,
    x_ref,
    top_ref,
    gain_ref,
    scale_ref,
    win_hbm,
    wout_hbm,
    act_ref,
    grad_ref,
    win,
    wout,
    x_in,
    y_out,
    g_in,
    g_out,
    normed,
    inv_std,
    slope,
    accum,
    pick_a,
    pick_g,
    rows_a,
    rows_g,
    send_a,
    send_g,
    recv_a,
    recv_g,
    sum_a,
    sum_g,
    zsend_a,
    zsend_g,
    zrecv_a,
    zrecv_g,
    w_sem,
    relay_s,
    relay_r,
    ga_s,
    ga_r,
    gg_s,
    gg_r,
    ra_s,
    ra_r,
    rg_s,
    rg_r,
    za_s,
    za_r,
    zg_s,
    zg_r,
):
    side = cube_side(dp_count)
    sec = lax.axis_index("section")
    me = lax.axis_index("dp")
    cx = me // (side * side)
    cz = lax.rem(me // side, side)
    cy = lax.rem(me, side)
    batches, rows, width = x_ref.shape
    hidden_width = win.shape[1]
    block_a = width // dp_count
    block_g = hidden_width // dp_count
    chunk = min(256, hidden_width)
    chunks = hidden_width // chunk
    total_rows = batches * rows * dp_count

    def index_of(px, pz, py):
        return px * side * side + pz * side + py

    def x_peer(k):
        return index_of(lax.rem(cx + k, side), cz, cy)

    def y_peer(k):
        return index_of(cx, cz, lax.rem(cy + k, side))

    def z_peer(k):
        return index_of(cx, lax.rem(cz + k, side), cy)

    def remote(src, dst, ssem, rsem, device):
        return pltpu.make_async_remote_copy(
            src_ref=src, dst_ref=dst, send_sem=ssem, recv_sem=rsem,
            device_id=device, device_id_type=MESH,
        )

    steps = range(1, side)
    load_in = pltpu.make_async_copy(win_hbm, win, w_sem.at[0])
    load_out = pltpu.make_async_copy(wout_hbm, wout, w_sem.at[1])
    load_in.start()
    load_out.start()

    barrier = pltpu.get_barrier_semaphore()
    for k in steps:
        for peer in (x_peer(k), y_peer(k), z_peer(k)):
            pl.semaphore_signal(barrier, inc=1, device_id=(peer, sec), device_id_type=MESH)

    for shift in (1, sections - 1):
        pl.semaphore_signal(
            barrier, inc=1, device_id=(me, lax.rem(sec + shift, sections)), device_id_type=MESH
        )

    def barrier_wait():
        pl.semaphore_wait(barrier, 3 * (side - 1) + 2)

    def build_picks():
        for pick, block in ((pick_a, block_a), (pick_g, block_g)):
            extent = pick.shape[2]
            offset = lax.broadcasted_iota(jnp.int32, (block, extent), 1) - lax.broadcasted_iota(
                jnp.int32, (block, extent), 0
            )
            for m in range(2):
                for q in range(side):
                    for zz in range(side):
                        owner = owner_ref[index_of(cx, zz, q) if m == 0 else index_of(q, zz, cy)]
                        row = (q * side + zz) * block
                        pick[m, row : row + block, :] = jnp.where(
                            offset == owner * block, 1.0, 0.0
                        ).astype(BF16)

    forward_copies = [
        remote(y_out.at[m], x_in.at[m], relay_s.at[m], relay_r.at[m], (me, lax.rem(sec + 1, sections)))
        for m in range(batches)
    ]
    backward_copies = [
        remote(
            g_out.at[m], g_in.at[m], relay_s.at[2 + m], relay_r.at[2 + m],
            (me, lax.rem(sec + sections - 1, sections)),
        )
        for m in range(batches)
    ]
    own = (cx, cy)

    def gather_copies(buffer, ssem, rsem):
        return [
            remote(
                buffer.at[m, own[m]], buffer.at[m, own[m]], ssem.at[m, k - 1], rsem.at[m, k - 1],
                (x_peer(k) if m == 0 else y_peer(k), sec),
            )
            for m in range(2)
            for k in steps
        ]

    gather_a = gather_copies(rows_a, ga_s, ga_r)
    gather_g = gather_copies(rows_g, gg_s, gg_r)

    def scatter_copy(send, recv, ssem, rsem, m, k):
        return remote(
            send.at[m, k - 1], recv.at[m, k - 1], ssem.at[m, k - 1], rsem.at[m, k - 1],
            (y_peer(k) if m == 0 else x_peer(k), sec),
        )

    def z_copy(send, recv, ssem, rsem, k):
        return remote(send.at[k - 1], recv.at[k - 1], ssem.at[k - 1], rsem.at[k - 1], (z_peer(k), sec))

    def products(rows_ref, pick, block, send, total, recv, ssem, rsem):
        span = side * block
        extent = rows_ref.shape[3]
        for k in list(steps)[::-1] + [0]:
            for m in range(2):
                axis = cy if m == 0 else cx
                dest = lax.rem(axis + k, side)
                gathered = rows_ref[m].reshape(side * rows, extent)
                chosen = pick[m, pl.ds(pl.multiple_of(dest * span, span), span), :]
                left = lax.dot_general(chosen, gathered, NT, preferred_element_type=F32).astype(BF16)
                part = jnp.dot(left, gathered, preferred_element_type=F32)
                if k:
                    send[m, k - 1] = part.astype(BF16)
                    scatter_copy(send, recv, ssem, rsem, m, k).start()
                elif m == 0:
                    total[...] = part
                else:
                    total[...] += part

    def collect(block, send, total, recv, zsend, zrecv, ssem, rsem, zs, zr):
        for k in steps:
            for m in range(2):
                scatter_copy(send, recv, ssem, rsem, m, k).wait_recv()
        value = total[...]
        for k in steps:
            for m in range(2):
                value = value + recv[m, k - 1].astype(F32)
        total[...] = value
        for k in steps:
            dest = lax.rem(cz + k, side)
            zsend[k - 1] = total[pl.ds(pl.multiple_of(dest * block, block), block), :].astype(BF16)
            z_copy(zsend, zrecv, zs, zr, k).start()

    def finish(block, total, zsend, zrecv, zs, zr, out):
        for k in steps:
            z_copy(zsend, zrecv, zs, zr, k).wait_recv()
        value = total[pl.ds(pl.multiple_of(cz * block, block), block), :]
        for k in steps:
            value = value + zrecv[k - 1].astype(F32)
        out[...] = value / total_rows

    gain = gain_ref[...]
    scales = scale_ref[...]

    @pl.when(sec > 0)
    def _():
        build_picks()
        for copy in forward_copies:
            copy.wait_recv()

    @pl.when(sec == 0)
    def _():
        x_in[...] = x_ref[...]

    floats = x_in[...].reshape(batches * rows, width).astype(F32)
    center = floats - jnp.mean(floats, axis=-1, keepdims=True)
    inverse = lax.rsqrt(jnp.mean(center * center, axis=-1, keepdims=True) + 1e-06)
    normal = center * inverse
    normed[...] = normal
    inv_std[...] = inverse
    scaled_rows = (normal * gain).astype(BF16)
    rows_a[0, cx] = scaled_rows[:rows]
    rows_a[1, cy] = scaled_rows[rows:]
    accum[...] = jnp.zeros_like(accum)
    load_in.wait()
    load_out.wait()
    for j in range(chunks):
        cols = slice(j * chunk, (j + 1) * chunk)
        hidden = jnp.dot(scaled_rows, win[:, cols], preferred_element_type=F32)
        cdf = 0.5 * (1.0 + lax.erf(hidden * SQRT_HALF))
        activated = (hidden * cdf).astype(BF16)
        slope[:, cols] = cdf + hidden * INV_ROOT_TAU * jnp.exp(-0.5 * hidden * hidden)
        accum[...] += jnp.dot(activated, wout[cols, :], preferred_element_type=F32)

    barrier_wait()

    @pl.when(sec < sections - 1)
    def _():
        for m in range(batches):
            part = slice(m * rows, (m + 1) * rows)
            y_out[m] = (x_in[m].astype(F32) + scales * accum[part, :]).astype(BF16)
            forward_copies[m].start()

    for copy in gather_a:
        copy.start()

    @pl.when(sec == 0)
    def _():
        build_picks()

    def first_a():
        for copy in gather_a:
            copy.wait_recv()
        products(rows_a, pick_a, block_a, send_a, sum_a, recv_a, ra_s, ra_r)

    @pl.when(sec < sections - 1)
    def _():
        first_a()

    @pl.when(sec < sections - 1)
    def _():
        for copy in backward_copies:
            copy.wait_recv()

    @pl.when(sec == sections - 1)
    def _():
        g_in[...] = top_ref[...]

    cot = g_in[...].reshape(batches * rows, width).astype(F32)
    gz = (cot * scales).astype(BF16)
    accum[...] = jnp.zeros_like(accum)
    for j in range(chunks):
        cols = slice(j * chunk, (j + 1) * chunk)
        grad_act = lax.dot_general(gz, wout[cols, :], NT, preferred_element_type=F32)
        grad_hidden = (grad_act * slope[:, cols]).astype(BF16)
        rows_g[0, cx, :, cols] = grad_hidden[:rows]
        rows_g[1, cy, :, cols] = grad_hidden[rows:]

        @pl.when(sec > 0)
        def _():
            accum[...] += lax.dot_general(
                grad_hidden, win[:, cols], NT, preferred_element_type=F32
            )

    @pl.when(sec > 0)
    def _():
        for m in range(batches):
            part = slice(m * rows, (m + 1) * rows)
            normal_part = normed[part, :]
            grad_normed = accum[part, :] * gain
            mean_one = jnp.mean(grad_normed, axis=-1, keepdims=True)
            mean_two = jnp.mean(grad_normed * normal_part, axis=-1, keepdims=True)
            grad_input = g_in[m].astype(F32) + inv_std[part, :] * (
                grad_normed - mean_one - normal_part * mean_two
            )
            g_out[m] = grad_input.astype(BF16)
            backward_copies[m].start()

    for copy in gather_g:
        copy.start()

    @pl.when(sec == sections - 1)
    def _():
        first_a()

    collect(block_a, send_a, sum_a, recv_a, zsend_a, zrecv_a, ra_s, ra_r, za_s, za_r)
    for copy in gather_g:
        copy.wait_recv()
    products(rows_g, pick_g, block_g, send_g, sum_g, recv_g, rg_s, rg_r)
    finish(block_a, sum_a, zsend_a, zrecv_a, za_s, za_r, act_ref)
    collect(block_g, send_g, sum_g, recv_g, zsend_g, zrecv_g, rg_s, rg_r, zg_s, zg_r)
    finish(block_g, sum_g, zsend_g, zrecv_g, zg_s, zg_r, grad_ref)

    @pl.when(sec < sections - 1)
    def _():
        for copy in forward_copies:
            copy.wait_send()

    @pl.when(sec > 0)
    def _():
        for copy in backward_copies:
            copy.wait_send()

    for copy in gather_a + gather_g:
        copy.wait_send()
    for k in steps:
        for m in range(2):
            scatter_copy(send_a, recv_a, ra_s, ra_r, m, k).wait_send()
            scatter_copy(send_g, recv_g, rg_s, rg_r, m, k).wait_send()
        z_copy(zsend_a, zrecv_a, za_s, za_r, k).wait_send()
        z_copy(zsend_g, zrecv_g, zg_s, zg_r, k).wait_send()


def body(dp_count, sections, inputs, ln_gain, w_in, w_out, layer_scale, out_grad, owner_table):
    batches, rows, width = inputs.shape
    hidden_width = w_in.shape[2]
    side = cube_side(dp_count)
    block_a = width // dp_count
    block_g = hidden_width // dp_count
    span_a, span_g = side * block_a, side * block_g
    tokens = batches * rows
    dma = pltpu.SemaphoreType.DMA
    vmem = pl.BlockSpec(memory_space=pltpu.VMEM)
    hbm = pl.BlockSpec(memory_space=pl.ANY)
    act, grad = pl.pallas_call(
        functools.partial(kernel, dp_count, sections),
        out_shape=(
            jax.ShapeDtypeStruct((block_a, width), F32),
            jax.ShapeDtypeStruct((block_g, hidden_width), F32),
        ),
        in_specs=[pl.BlockSpec(memory_space=pltpu.SMEM), vmem, vmem, vmem, vmem, hbm, hbm],
        out_specs=(vmem, vmem),
        scratch_shapes=[
            pltpu.VMEM((width, hidden_width), BF16),
            pltpu.VMEM((hidden_width, width), BF16),
            pltpu.VMEM((batches, rows, width), BF16),
            pltpu.VMEM((batches, rows, width), BF16),
            pltpu.VMEM((batches, rows, width), BF16),
            pltpu.VMEM((batches, rows, width), BF16),
            pltpu.VMEM((tokens, width), F32),
            pltpu.VMEM((tokens, 1), F32),
            pltpu.VMEM((tokens, hidden_width), F32),
            pltpu.VMEM((tokens, width), F32),
            pltpu.VMEM((2, side * span_a, width), BF16),
            pltpu.VMEM((2, side * span_g, hidden_width), BF16),
            pltpu.VMEM((2, side, rows, width), BF16),
            pltpu.VMEM((2, side, rows, hidden_width), BF16),
            pltpu.VMEM((2, side - 1, span_a, width), BF16),
            pltpu.VMEM((2, side - 1, span_g, hidden_width), BF16),
            pltpu.VMEM((2, side - 1, span_a, width), BF16),
            pltpu.VMEM((2, side - 1, span_g, hidden_width), BF16),
            pltpu.VMEM((span_a, width), F32),
            pltpu.VMEM((span_g, hidden_width), F32),
            pltpu.VMEM((side - 1, block_a, width), BF16),
            pltpu.VMEM((side - 1, block_g, hidden_width), BF16),
            pltpu.VMEM((side - 1, block_a, width), BF16),
            pltpu.VMEM((side - 1, block_g, hidden_width), BF16),
            dma((2,)),
            dma((4,)),
            dma((4,)),
        ]
        + [dma((2, side - 1)) for _ in range(8)]
        + [dma((side - 1,)) for _ in range(4)],
        compiler_params=pltpu.CompilerParams(
            collective_id=0, has_side_effects=True, vmem_limit_bytes=60 * 1024 * 1024
        ),
        name="window",
    )(owner_table, inputs, out_grad, ln_gain, layer_scale, w_in[0], w_out[0])
    return (act[None], grad[None])


def solution(mesh):
    placed = (
        P(None, "dp", None),
        P("section", None),
        P("section", None, None),
        P("section", None, None),
        P("section", None),
        P(None, "dp", None),
        P(),
    )
    return jax.shard_map(
        functools.partial(body, mesh.shape["dp"], mesh.shape["section"]),
        mesh=mesh,
        in_specs=placed,
        out_specs=(P("section", "dp", None), P("section", "dp", None)),
        check_vma=False,
    )
```

time: 896 us -> 108 us (0.12)
  waiting for transfers between devices: 789 us -> 0 us
  Pallas kernels: 0 us -> 104 us
  matrix products: 48 us -> 0 us
  starting transfers between devices: 22.5 us -> 0 us
  between operations: 14.8 us -> 0.64 us
    reduce_scatter x2 -> x0, waiting for transfers between devices: 764 us -> none  [the longest x1 437 us: body(): lax.psum_scatter(square_term(grad_perm, grad_rows, total_rows), 'dp', sca...]
    pallas_call x0 -> x1, Pallas kernels: none -> 104 us  [body(): pl.pallas_call(functools.partial(kernel, dp_count, sections), out_shape=(...]
    dot_general x20 -> x0, matrix products: 48 us -> none  [the longest x5 15.9 us: backward_block(): lax.dot_general(scaled, weight_out, (((1,), (1,)), ((), ())), preferred_e...]
    ppermute x8 -> x0, waiting for transfers between devices: 24.6 us -> none  [passed_along(): lax.ppermute(value, axis, [(source, source + steps) for source in range(i...]
    ppermute x8 -> x0, starting transfers between devices: 22.4 us -> none  [passed_along(): lax.ppermute(value, axis, [(source, source + steps) for source in range(i...]
  transfers between devices with their start and end apart: 10 -> 0, of which waited for: 9 -> 0; matrix products, arithmetic and copies ran while one was open for 5% -> 0% of each run, Pallas kernels for 0% -> 0%
where the time goes in v1:
time: 108 us
  Pallas kernels  104 us (96%)
  local copies, waits for them, and re-layouts  3.14 us (3%)
    pallas_call x1, Pallas kernels, body(): pl.pallas_call(functools.partial(kernel, dp_count, sections), out_shape=(...  104 us
    unnamed x2, local copies, waits for them, and re-layouts  3.14 us

profile of v1, /device:TPU:8, one launch (start us, length us, event | category | flops | bytes accessed | tf_op | source)
XLA Modules:
  0.0 108.0 jit_solution(5664719533689877314)
XLA Ops:
  0.6 104.3 %window.1 = (f32[16,1024]{1,0:T(8,128)}, f32[32,2048]{1,0:T(8,128)}) custom-call(s32[64]{0:T(128)} %owner_ref.1, bf16[2,64,1024]{2,1,0:T(8,128)(2,1)} %x_ref.1, bf16[2,64,1024]{2,1,0:T(8,128)(2,1)} %top_ref.1, f32[1,1024]{1,0:T(1,128)} %gain_ref.1, f32[1,1024]{1,0:T(1,128)} %scale_ref.1, bf16[1024,2048]{1,0:T(8,128)(2,1)} %bitcast.4, bf16[2048,1024]{1,0:T(8,128)(2,1)} %bitcast.5), custom_call_target="tpu_custom_call" | custom-call | tf_op jit(solution)/shard_map/window/pallas_call | solution.py:361
  104.9 1.5 %copy.11 = f32[1,16,1024]{2,1,0:T(8,128)} copy(f32[1,16,1024]{2,1,0:T(8,128)} %bitcast.7) | data formatting | bytes 131072
  106.4 1.7 %copy.12 = f32[1,32,2048]{2,1,0:T(8,128)} copy(f32[1,32,2048]{2,1,0:T(8,128)} %bitcast.6) | data formatting | bytes 524288

commit v2 on v1

v2 whole, which is shorter than its diff:
```python
import functools
import jax
import jax.numpy as jnp
from jax import lax
from jax.experimental import pallas as pl
from jax.experimental.pallas import tpu as pltpu
from jax.sharding import PartitionSpec as P

SQRT_HALF = 0.7071067811865476
INV_ROOT_TAU = 0.3989422804014327
MESH = pl.DeviceIdType.MESH
F32 = jnp.float32
BF16 = jnp.bfloat16
NT = (((1,), (1,)), ((), ()))


RING = 4
HALVES = 2


def kernel(
    dp_count,
    sections,
    owner_ref,
    x_hbm,
    top_hbm,
    gain_ref,
    scale_ref,
    win_hbm,
    wout_hbm,
    act_ref,
    grad_ref,
    win,
    wout,
    x_in,
    y_out,
    g_in,
    g_out,
    normed,
    inv_std,
    slope,
    accum,
    *rest,
):
    (pick_a, rows_a, left_a, far_a, near_a, hold_a, sum_a, far_in_a, near_in_a, zs_a, zr_a) = rest[:11]
    (pick_g, rows_g, left_g, far_g, near_g, hold_g, sum_g, far_in_g, near_in_g, zs_g, zr_g) = rest[11:22]
    (w_sem, io_sem, relay_s, relay_r, gat_s, gat_r, sca_s, sca_r, z_s, z_r) = rest[22:]
    planes = dp_count // (RING * RING)
    sec = lax.axis_index("section")
    me = lax.axis_index("dp")
    cx = me // (planes * RING)
    cz = lax.rem(me // RING, planes)
    cy = lax.rem(me, RING)
    even = lax.rem(sec, 2) == 0
    batches, rows, width = x_in.shape
    tokens = batches * rows
    hidden_width = win.shape[1]
    block_a = width // dp_count
    block_g = hidden_width // dp_count
    chunk = min(256, hidden_width // HALVES)
    chunks = hidden_width // chunk
    total_rows = tokens * dp_count

    def index_of(px, pz, py):
        return px * planes * RING + pz * RING + py

    p = jnp.where(even, cx, cy)
    q = jnp.where(even, cy, cx)

    def at_pq(pp, pz, qq):
        return index_of(jnp.where(even, pp, qq), pz, jnp.where(even, qq, pp))

    def ring(value, k):
        return lax.rem(value + k + RING, RING)

    def p_peer(k):
        return (at_pq(ring(p, k), cz, q), sec)

    def q_peer(k):
        return (at_pq(p, cz, ring(q, k)), sec)

    def z_peer(k):
        return (index_of(cx, lax.rem(cz + k, planes), cy), sec)

    def remote(src, dst, ssem, rsem, device):
        return pltpu.make_async_remote_copy(
            src_ref=src, dst_ref=dst, send_sem=ssem, recv_sem=rsem,
            device_id=device, device_id_type=MESH,
        )

    load_in = []
    load_out = []
    for j in range(chunks):
        cols = pl.ds(j * chunk, chunk)
        load_in.append(pltpu.make_async_copy(win_hbm.at[:, cols], win.at[:, cols], w_sem.at[0, j]))
        load_out.append(pltpu.make_async_copy(wout_hbm.at[cols, :], wout.at[cols, :], w_sem.at[1, j]))
    load_x = pltpu.make_async_copy(x_hbm, x_in, io_sem.at[0])
    load_top = pltpu.make_async_copy(top_hbm, g_in, io_sem.at[1])

    @pl.when(sec == 0)
    def _():
        load_x.start()

    for j in range(chunks):
        load_in[j].start()
        load_out[j].start()

    @pl.when(sec == sections - 1)
    def _():
        load_top.start()

    barrier = pltpu.get_barrier_semaphore()
    greeted = [p_peer(1), p_peer(-1), q_peer(1), q_peer(-1)]
    greeted += [z_peer(k) for k in range(1, planes)]
    greeted += [(me, lax.rem(sec + 1, sections)), (me, lax.rem(sec + sections - 1, sections))]
    for device in greeted:
        pl.semaphore_signal(barrier, inc=1, device_id=device, device_id_type=MESH)

    def build_picks():
        for pick, block in ((pick_a, block_a), (pick_g, block_g)):
            extent = pick.shape[1]
            offset = lax.broadcasted_iota(jnp.int32, (block, extent), 1) - lax.broadcasted_iota(
                jnp.int32, (block, extent), 0
            )
            for qq in range(RING):
                for zz in range(planes):
                    owner = owner_ref[at_pq(p, zz, qq)]
                    row = (qq * planes + zz) * block
                    pick[row : row + block, :] = jnp.where(offset == owner * block, 1.0, 0.0).astype(BF16)

    forward_copies = [
        remote(y_out.at[m], x_in.at[m], relay_s.at[m], relay_r.at[m], (me, lax.rem(sec + 1, sections)))
        for m in range(batches)
    ]
    backward_copies = [
        remote(
            g_out.at[m], g_in.at[m], relay_s.at[batches + m], relay_r.at[batches + m],
            (me, lax.rem(sec + sections - 1, sections)),
        )
        for m in range(batches)
    ]

    class Factor:
        pass

    def factor(number, block, groups, pick, buffers):
        f = Factor()
        f.block, f.span, f.groups, f.pick = block, planes * block, groups, pick
        (f.rows, f.left, f.far, f.near, f.hold, f.total, f.far_in, f.near_in, f.zs, f.zr) = buffers
        f.half = f.far.shape[3]
        gs, gr = gat_s.at[number], gat_r.at[number]

        def row_copy(slot, h, n, k):
            return remote(f.rows.at[h, slot], f.rows.at[h, slot], gs.at[n], gr.at[n], p_peer(k))

        f.send_half = [[row_copy(p, h, h, 1), row_copy(p, h, 3 + h, -1)] for h in range(HALVES)]
        f.pass_on = [row_copy(ring(p, -1), 0, 2, 1), row_copy(ring(p, 1), 1, 5, -1)]
        f.gathers = [c for pair in f.send_half for c in pair] + f.pass_on
        ss, sr = sca_s.at[number], sca_r.at[number]
        f.far_copy = [
            [
                remote(f.far.at[g, d], f.far_in.at[g, d], ss.at[g, d], sr.at[g, d], q_peer((1, -1)[d]))
                for d in range(2)
            ]
            for g in range(groups)
        ]
        f.near_copy = [
            [
                [
                    remote(
                        f.near.at[g, d, h], f.near_in.at[g, d, h], ss.at[g, 2 + 2 * d + h],
                        sr.at[g, 2 + 2 * d + h], q_peer((1, -1)[d]),
                    )
                    for h in range(2)
                ]
                for d in range(2)
            ]
            for g in range(groups)
        ]
        f.z_copy = [
            [
                remote(
                    f.zs.at[g, k - 1], f.zr.at[g, k - 1], z_s.at[number, g, k - 1],
                    z_r.at[number, g, k - 1], z_peer(k),
                )
                for k in range(1, planes)
            ]
            for g in range(groups)
        ]
        return f

    fa = factor(0, block_a, 1, pick_a, (rows_a, left_a, far_a, near_a, hold_a, sum_a, far_in_a, near_in_a, zs_a, zr_a))
    fg = factor(1, block_g, 2, pick_g, (rows_g, left_g, far_g, near_g, hold_g, sum_g, far_in_g, near_in_g, zs_g, zr_g))

    def start_half(f, h):
        for copy in f.send_half[h]:
            copy.start()

    def finish_gather(f):
        f.send_half[0][0].wait_recv()
        f.pass_on[0].start()
        f.send_half[1][1].wait_recv()
        f.pass_on[1].start()
        f.send_half[0][1].wait_recv()
        f.send_half[1][0].wait_recv()
        f.pass_on[0].wait_recv()
        f.pass_on[1].wait_recv()

    def choose(f):
        extent = f.rows.shape[3]
        picked = None
        for h in range(HALVES):
            source = f.rows[h].reshape(RING * tokens, extent)
            part = lax.dot_general(
                f.pick[:, h * extent : (h + 1) * extent], source, NT, preferred_element_type=F32
            )
            picked = part if picked is None else picked + part
        f.left[...] = picked.astype(BF16)

    def part_of(f, g, k):
        extent = f.rows.shape[3]
        dest = ring(q, k)
        left = f.left[pl.ds(pl.multiple_of(dest * f.span, f.span), f.span), :]
        pieces = [
            jnp.dot(left, f.rows[h].reshape(RING * tokens, extent), preferred_element_type=F32)
            for h in ((g,) if f.groups == 2 else range(HALVES))
        ]
        return pieces[0] if len(pieces) == 1 else jnp.concatenate(pieces, axis=1)

    def far_part(f, g):
        part = part_of(f, g, 2)
        for d in range(2):
            f.far[g, d] = part[:, d * f.half : (d + 1) * f.half].astype(BF16)
            f.far_copy[g][d].start()

    def near_part(f, g, d):
        part = part_of(f, g, (1, -1)[d])
        free = 1 - d
        f.near[g, d, free] = part[:, free * f.half : (free + 1) * f.half].astype(BF16)
        f.near_copy[g][d][free].start()
        f.hold[g, d] = part[:, d * f.half : (d + 1) * f.half]

    def own_part(f, g):
        f.total[g] = part_of(f, g, 0)

    def relay_part(f, g):
        for d in range(2):
            f.far_copy[g][d].wait_recv()
            f.near[g, d, d] = (f.hold[g, d] + f.far_in[g, d].astype(F32)).astype(BF16)
            f.near_copy[g][d][d].start()

    def collect(f, g):
        for d in range(2):
            for h in range(2):
                f.near_copy[g][d][h].wait_recv()
        for h in range(2):
            cols = slice(h * f.half, (h + 1) * f.half)
            f.total[g, :, cols] += f.near_in[g, 0, h].astype(F32) + f.near_in[g, 1, h].astype(F32)
        for k in range(1, planes):
            dest = lax.rem(cz + k, planes)
            f.zs[g, k - 1] = f.total[g, pl.ds(pl.multiple_of(dest * f.block, f.block), f.block), :].astype(BF16)
            f.z_copy[g][k - 1].start()

    def finish(f, g, out):
        for copy in f.z_copy[g]:
            copy.wait_recv()
        value = f.total[g, pl.ds(pl.multiple_of(cz * f.block, f.block), f.block), :]
        for k in range(1, planes):
            value = value + f.zr[g, k - 1].astype(F32)
        out[:, g * 2 * f.half : (g + 1) * 2 * f.half] = value / total_rows

    def act_products():
        finish_gather(fa)
        choose(fa)
        far_part(fa, 0)
        near_part(fa, 0, 0)
        near_part(fa, 0, 1)
        own_part(fa, 0)
        relay_part(fa, 0)

    gain = gain_ref[...]
    scales = scale_ref[...]

    @pl.when(sec > 0)
    def _():
        build_picks()
        for j in range(chunks):
            load_in[j].wait()
            load_out[j].wait()
        for copy in forward_copies:
            copy.wait_recv()

    @pl.when(sec == 0)
    def _():
        load_x.wait()

    floats = x_in[...].reshape(tokens, width).astype(F32)
    center = floats - jnp.mean(floats, axis=-1, keepdims=True)
    inverse = lax.rsqrt(jnp.mean(center * center, axis=-1, keepdims=True) + 1e-06)
    normal = center * inverse
    normed[...] = normal
    inv_std[...] = inverse
    half_a = width // HALVES
    scaled_rows = (normal * gain).astype(BF16)
    for h in range(HALVES):
        rows_a[h, p] = scaled_rows[:, h * half_a : (h + 1) * half_a]

    def forward_chunk(j, scaled):
        cols = slice(j * chunk, (j + 1) * chunk)
        hidden = jnp.dot(scaled, win[:, cols], preferred_element_type=F32)
        cdf = 0.5 * (1.0 + lax.erf(hidden * SQRT_HALF))
        activated = (hidden * cdf).astype(BF16)
        slope[:, cols] = cdf + hidden * INV_ROOT_TAU * jnp.exp(-0.5 * hidden * hidden)
        part = jnp.dot(activated, wout[cols, :], preferred_element_type=F32)
        if j:
            accum[...] += part
        else:
            accum[...] = part

    @pl.when(sec == 0)
    def _():
        scaled = jnp.concatenate([rows_a[h, p] for h in range(HALVES)], axis=1)
        for j in range(chunks):
            load_in[j].wait()
            load_out[j].wait()
            forward_chunk(j, scaled)

    @pl.when(sec > 0)
    def _():
        scaled = jnp.concatenate([rows_a[h, p] for h in range(HALVES)], axis=1)
        for j in range(chunks):
            forward_chunk(j, scaled)

    pl.semaphore_wait(barrier, len(greeted))

    @pl.when(sec < sections - 1)
    def _():
        for m in range(batches):
            part = slice(m * rows, (m + 1) * rows)
            y_out[m] = (x_in[m].astype(F32) + scales * accum[part, :]).astype(BF16)
            forward_copies[m].start()

    for h in range(HALVES):
        start_half(fa, h)

    @pl.when(sec == 0)
    def _():
        build_picks()

    @pl.when(sec < sections // 2)
    def _():
        act_products()
        collect(fa, 0)

    @pl.when(sec < sections - 1)
    def _():
        for copy in backward_copies:
            copy.wait_recv()

    @pl.when(sec == sections - 1)
    def _():
        load_top.wait()

    def backward_chunk(j, gz, onward):
        cols = slice(j * chunk, (j + 1) * chunk)
        grad_act = lax.dot_general(gz, wout[cols, :], NT, preferred_element_type=F32)
        grad_hidden = (grad_act * slope[:, cols]).astype(BF16)
        per = chunks // HALVES
        h, inner = j // per, j % per
        rows_g[h, p, :, inner * chunk : (inner + 1) * chunk] = grad_hidden
        if onward:
            part = lax.dot_general(grad_hidden, win[:, cols], NT, preferred_element_type=F32)
            if j:
                accum[...] += part
            else:
                accum[...] = part
        if inner == per - 1:
            start_half(fg, h)

    @pl.when(sec == 0)
    def _():
        gz = (g_in[...].reshape(tokens, width).astype(F32) * scales).astype(BF16)
        for j in range(chunks):
            backward_chunk(j, gz, False)

    @pl.when(sec > 0)
    def _():
        gz = (g_in[...].reshape(tokens, width).astype(F32) * scales).astype(BF16)
        for j in range(chunks):
            backward_chunk(j, gz, True)
        for m in range(batches):
            part = slice(m * rows, (m + 1) * rows)
            normal_part = normed[part, :]
            grad_normed = accum[part, :] * gain
            mean_one = jnp.mean(grad_normed, axis=-1, keepdims=True)
            mean_two = jnp.mean(grad_normed * normal_part, axis=-1, keepdims=True)
            grad_input = g_in[m].astype(F32) + inv_std[part, :] * (
                grad_normed - mean_one - normal_part * mean_two
            )
            g_out[m] = grad_input.astype(BF16)
            backward_copies[m].start()

    finish_gather(fg)
    choose(fg)
    far_part(fg, 0)
    near_part(fg, 0, 0)
    near_part(fg, 0, 1)
    far_part(fg, 1)
    relay_part(fg, 0)
    near_part(fg, 1, 0)
    near_part(fg, 1, 1)
    own_part(fg, 0)
    relay_part(fg, 1)
    own_part(fg, 1)
    collect(fg, 0)

    @pl.when(sec >= sections // 2)
    def _():
        act_products()
        collect(fa, 0)

    collect(fg, 1)
    finish(fa, 0, act_ref)
    finish(fg, 0, grad_ref)
    finish(fg, 1, grad_ref)

    @pl.when(sec < sections - 1)
    def _():
        for copy in forward_copies:
            copy.wait_send()

    @pl.when(sec > 0)
    def _():
        for copy in backward_copies:
            copy.wait_send()

    for f in (fa, fg):
        for copy in f.gathers:
            copy.wait_send()
        for g in range(f.groups):
            for d in range(2):
                f.far_copy[g][d].wait_send()
                for h in range(2):
                    f.near_copy[g][d][h].wait_send()
            for copy in f.z_copy[g]:
                copy.wait_send()


def body(dp_count, sections, inputs, ln_gain, w_in, w_out, layer_scale, out_grad, owner_table):
    batches, rows, width = inputs.shape
    hidden_width = w_in.shape[2]
    planes = dp_count // (RING * RING)
    block_a = width // dp_count
    block_g = hidden_width // dp_count
    tokens = batches * rows
    chunk = min(256, hidden_width // HALVES)
    dma = pltpu.SemaphoreType.DMA
    vmem = pl.BlockSpec(memory_space=pltpu.VMEM)
    hbm = pl.BlockSpec(memory_space=pl.ANY)

    def factor_scratch(block, extent, groups):
        span = planes * block
        half = extent // groups // 2
        others = max(planes - 1, 1)
        return [
            pltpu.VMEM((RING * span, extent), BF16),
            pltpu.VMEM((HALVES, RING, tokens, extent // HALVES), BF16),
            pltpu.VMEM((RING * span, RING * tokens), BF16),
            pltpu.VMEM((groups, 2, span, half), BF16),
            pltpu.VMEM((groups, 2, 2, span, half), BF16),
            pltpu.VMEM((groups, 2, span, half), F32),
            pltpu.VMEM((groups, span, 2 * half), F32),
            pltpu.VMEM((groups, 2, span, half), BF16),
            pltpu.VMEM((groups, 2, 2, span, half), BF16),
            pltpu.VMEM((groups, others, block, 2 * half), BF16),
            pltpu.VMEM((groups, others, block, 2 * half), BF16),
        ]

    act, grad = pl.pallas_call(
        functools.partial(kernel, dp_count, sections),
        out_shape=(
            jax.ShapeDtypeStruct((block_a, width), F32),
            jax.ShapeDtypeStruct((block_g, hidden_width), F32),
        ),
        in_specs=[pl.BlockSpec(memory_space=pltpu.SMEM), hbm, hbm, vmem, vmem, hbm, hbm],
        out_specs=(vmem, vmem),
        scratch_shapes=[
            pltpu.VMEM((width, hidden_width), BF16),
            pltpu.VMEM((hidden_width, width), BF16),
            pltpu.VMEM((batches, rows, width), BF16),
            pltpu.VMEM((batches, rows, width), BF16),
            pltpu.VMEM((batches, rows, width), BF16),
            pltpu.VMEM((batches, rows, width), BF16),
            pltpu.VMEM((tokens, width), F32),
            pltpu.VMEM((tokens, 1), F32),
            pltpu.VMEM((tokens, hidden_width), F32),
            pltpu.VMEM((tokens, width), F32),
        ]
        + factor_scratch(block_a, width, 1)
        + factor_scratch(block_g, hidden_width, 2)
        + [
            dma((2, hidden_width // chunk)),
            dma((2,)),
            dma((2 * batches,)),
            dma((2 * batches,)),
            dma((2, 6)),
            dma((2, 6)),
            dma((2, 2, 6)),
            dma((2, 2, 6)),
            dma((2, 2, max(planes - 1, 1))),
            dma((2, 2, max(planes - 1, 1))),
        ],
        compiler_params=pltpu.CompilerParams(
            collective_id=0, has_side_effects=True, vmem_limit_bytes=60 * 1024 * 1024
        ),
        name="window",
    )(owner_table, inputs, out_grad, ln_gain, layer_scale, w_in[0], w_out[0])
    return (act[None], grad[None])


def solution(mesh):
    placed = (
        P(None, "dp", None),
        P("section", None),
        P("section", None, None),
        P("section", None, None),
        P("section", None),
        P(None, "dp", None),
        P(),
    )
    return jax.shard_map(
        functools.partial(body, mesh.shape["dp"], mesh.shape["section"]),
        mesh=mesh,
        in_specs=placed,
        out_specs=(P("section", "dp", None), P("section", "dp", None)),
        check_vma=False,
    )
```

time: 108 us -> 86 us (0.80)
  Pallas kernels: 104 us -> 82 us
    pallas_call x1, Pallas kernels: 104 us -> 82 us  [body(): pl.pallas_call(functools.partial(kernel, dp_count, sections), out_shape=(...]
where the time goes in v2:
time: 86 us; the launch traced here: 85.8 us
  Pallas kernels  82 us (95%)
  local copies, waits for them, and re-layouts  3.14 us (4%)
    pallas_call x1, Pallas kernels, body(): pl.pallas_call(functools.partial(kernel, dp_count, sections), out_shape=(...  82 us
    unnamed x2, local copies, waits for them, and re-layouts  3.14 us

profile of v2, /device:TPU:8, one launch (start us, length us, event | category | flops | bytes accessed | tf_op | source)
XLA Modules:
  0.0 85.8 jit_solution(714535739727684748)
XLA Ops:
  0.6 82.0 %window.1 = (f32[16,1024]{1,0:T(8,128)}, f32[32,2048]{1,0:T(8,128)}) custom-call(s32[64]{0:T(128)} %owner_ref.1, bf16[2,64,1024]{2,1,0:T(8,128)(2,1)} %x_hbm.1, bf16[2,64,1024]{2,1,0:T(8,128)(2,1)} %top_hbm.1, f32[1,1024]{1,0:T(1,128)} %gain_ref.1, f32[1,1024]{1,0:T(1,128)} %scale_ref.1, bf16[1024,2048]{1,0:T(8,128)(2,1)} %bitcast.4, bf16[2048,1024]{1,0:T(8,128)(2,1)} %bitcast.5), custom_call_target="tpu_custom_call" | custom-call | tf_op jit(solution)/shard_map/window/pallas_call | solution.py:479
  82.7 1.5 %copy.11 = f32[1,16,1024]{2,1,0:T(8,128)} copy(f32[1,16,1024]{2,1,0:T(8,128)} %bitcast.7) | data formatting | bytes 131072
  84.2 1.7 %copy.12 = f32[1,32,2048]{2,1,0:T(8,128)} copy(f32[1,32,2048]{2,1,0:T(8,128)} %bitcast.6) | data formatting | bytes 524288

commit v3 on v2

--- a/solution.py
+++ b/solution.py
@@ -40,6 +40,7 @@
     inv_std,
     slope,
     accum,
+    acted,
     *rest,
 ):
     (pick_a, rows_a, left_a, far_a, near_a, hold_a, sum_a, far_in_a, near_in_a, zs_a, zr_a) = rest[:11]
@@ -52,14 +53,14 @@
     cz = lax.rem(me // RING, planes)
     cy = lax.rem(me, RING)
     even = lax.rem(sec, 2) == 0
-    batches, rows, width = x_in.shape
+    _, batches, rows, half_width = x_in.shape
+    width = HALVES * half_width
     tokens = batches * rows
     hidden_width = win.shape[1]
     block_a = width // dp_count
     block_g = hidden_width // dp_count
     chunk = min(256, hidden_width // HALVES)
     chunks = hidden_width // chunk
-    total_rows = tokens * dp_count
 
     def index_of(px, pz, py):
         return px * planes * RING + pz * RING + py
@@ -94,20 +95,30 @@
         cols = pl.ds(j * chunk, chunk)
         load_in.append(pltpu.make_async_copy(win_hbm.at[:, cols], win.at[:, cols], w_sem.at[0, j]))
         load_out.append(pltpu.make_async_copy(wout_hbm.at[cols, :], wout.at[cols, :], w_sem.at[1, j]))
-    load_x = pltpu.make_async_copy(x_hbm, x_in, io_sem.at[0])
-    load_top = pltpu.make_async_copy(top_hbm, g_in, io_sem.at[1])
+    load_x = []
+    load_top = []
+    for h in range(HALVES):
+        cols = pl.ds(h * half_width, half_width)
+        for m in range(batches):
+            load_x.append(
+                pltpu.make_async_copy(x_hbm.at[m, :, cols], x_in.at[h, m], io_sem.at[0, h * batches + m])
+            )
+            load_top.append(
+                pltpu.make_async_copy(top_hbm.at[m, :, cols], g_in.at[h, m], io_sem.at[1, h * batches + m])
+            )
 
     @pl.when(sec == 0)
     def _():
-        load_x.start()
-
-    for j in range(chunks):
-        load_in[j].start()
-        load_out[j].start()
+        for copy in load_x:
+            copy.start()
+
+    for copy in load_in + load_out:
+        copy.start()
 
     @pl.when(sec == sections - 1)
     def _():
-        load_top.start()
+        for copy in load_top:
+            copy.start()
 
     barrier = pltpu.get_barrier_semaphore()
     greeted = [p_peer(1), p_peer(-1), q_peer(1), q_peer(-1)]
@@ -129,15 +140,15 @@
                     pick[row : row + block, :] = jnp.where(offset == owner * block, 1.0, 0.0).astype(BF16)
 
     forward_copies = [
-        remote(y_out.at[m], x_in.at[m], relay_s.at[m], relay_r.at[m], (me, lax.rem(sec + 1, sections)))
-        for m in range(batches)
+        remote(y_out.at[h], x_in.at[h], relay_s.at[h], relay_r.at[h], (me, lax.rem(sec + 1, sections)))
+        for h in range(HALVES)
     ]
     backward_copies = [
         remote(
-            g_out.at[m], g_in.at[m], relay_s.at[batches + m], relay_r.at[batches + m],
+            g_out.at[h], g_in.at[h], relay_s.at[HALVES + h], relay_r.at[HALVES + h],
             (me, lax.rem(sec + sections - 1, sections)),
         )
-        for m in range(batches)
+        for h in range(HALVES)
     ]
 
     class Factor:
@@ -150,12 +161,18 @@
         f.half = f.far.shape[3]
         gs, gr = gat_s.at[number], gat_r.at[number]
 
-        def row_copy(slot, h, n, k):
-            return remote(f.rows.at[h, slot], f.rows.at[h, slot], gs.at[n], gr.at[n], p_peer(k))
-
-        f.send_half = [[row_copy(p, h, h, 1), row_copy(p, h, 3 + h, -1)] for h in range(HALVES)]
-        f.pass_on = [row_copy(ring(p, -1), 0, 2, 1), row_copy(ring(p, 1), 1, 5, -1)]
-        f.gathers = [c for pair in f.send_half for c in pair] + f.pass_on
+        def row_copy(slot, h, part, n, k):
+            piece = f.rows.at[h, slot]
+            if part is not None:
+                piece = f.rows.at[h, slot, pl.ds(part * (tokens // 2), tokens // 2)]
+            return remote(piece, piece, gs.at[n], gr.at[n], p_peer(k))
+
+        before, after = ring(p, -1), ring(p, 1)
+        f.plus = [row_copy(p, 0, None, 0, 1), row_copy(p, 1, None, 1, 1), row_copy(before, 0, None, 2, 1)]
+        f.minus = [row_copy(p, 0, None, 3, -1)]
+        f.minus += [row_copy(p, 1, i, 4 + i, -1) for i in range(2)]
+        f.minus += [row_copy(after, 1, i, 6 + i, -1) for i in range(2)]
+        f.gathers = f.plus + f.minus
         ss, sr = sca_s.at[number], sca_r.at[number]
         f.far_copy = [
             [
@@ -193,29 +210,43 @@
     fg = factor(1, block_g, 2, pick_g, (rows_g, left_g, far_g, near_g, hold_g, sum_g, far_in_g, near_in_g, zs_g, zr_g))
 
     def start_half(f, h):
-        for copy in f.send_half[h]:
-            copy.start()
-
-    def finish_gather(f):
-        f.send_half[0][0].wait_recv()
-        f.pass_on[0].start()
-        f.send_half[1][1].wait_recv()
-        f.pass_on[1].start()
-        f.send_half[0][1].wait_recv()
-        f.send_half[1][0].wait_recv()
-        f.pass_on[0].wait_recv()
-        f.pass_on[1].wait_recv()
-
-    def choose(f):
+        f.plus[h].start()
+        if h == 0:
+            f.minus[0].start()
+        else:
+            f.minus[1].start()
+            f.minus[2].start()
+
+    def choose(f, sources):
         extent = f.rows.shape[3]
         picked = None
         for h in range(HALVES):
-            source = f.rows[h].reshape(RING * tokens, extent)
+            pieces = [f.rows[h, source] for source in sources]
+            piece = pieces[0] if len(pieces) == 1 else jnp.concatenate(pieces, axis=0)
             part = lax.dot_general(
-                f.pick[:, h * extent : (h + 1) * extent], source, NT, preferred_element_type=F32
+                f.pick[:, h * extent : (h + 1) * extent], piece, NT, preferred_element_type=F32
             )
             picked = part if picked is None else picked + part
-        f.left[...] = picked.astype(BF16)
+        for i, source in enumerate(sources):
+            f.left[:, pl.ds(pl.multiple_of(source * tokens, tokens), tokens)] = picked[
+                :, i * tokens : (i + 1) * tokens
+            ].astype(BF16)
+
+    def finish_gather(f):
+        choose(f, [p])
+        f.plus[0].wait_recv()
+        f.plus[2].start()
+        f.minus[1].wait_recv()
+        f.minus[3].start()
+        f.minus[2].wait_recv()
+        f.minus[4].start()
+        f.plus[1].wait_recv()
+        f.minus[0].wait_recv()
+        choose(f, [ring(p, -1), ring(p, 1)])
+        f.plus[2].wait_recv()
+        f.minus[3].wait_recv()
+        f.minus[4].wait_recv()
+        choose(f, [ring(p, 2)])
 
     def part_of(f, g, k):
         extent = f.rows.shape[3]
@@ -267,11 +298,10 @@
         value = f.total[g, pl.ds(pl.multiple_of(cz * f.block, f.block), f.block), :]
         for k in range(1, planes):
             value = value + f.zr[g, k - 1].astype(F32)
-        out[:, g * 2 * f.half : (g + 1) * 2 * f.half] = value / total_rows
+        out[:, g * 2 * f.half : (g + 1) * 2 * f.half] = value
 
     def act_products():
         finish_gather(fa)
-        choose(fa)
         far_part(fa, 0)
         near_part(fa, 0, 0)
         near_part(fa, 0, 1)
@@ -284,46 +314,44 @@
     @pl.when(sec > 0)
     def _():
         build_picks()
-        for j in range(chunks):
-            load_in[j].wait()
-            load_out[j].wait()
+        for copy in load_in + load_out:
+            copy.wait()
         for copy in forward_copies:
             copy.wait_recv()
 
     @pl.when(sec == 0)
     def _():
-        load_x.wait()
-
-    floats = x_in[...].reshape(tokens, width).astype(F32)
+        for copy in load_x:
+            copy.wait()
+
+    def joined(ref):
+        return jnp.concatenate([ref[h].reshape(tokens, half_width) for h in range(HALVES)], axis=1)
+
+    floats = joined(x_in).astype(F32)
     center = floats - jnp.mean(floats, axis=-1, keepdims=True)
     inverse = lax.rsqrt(jnp.mean(center * center, axis=-1, keepdims=True) + 1e-06)
     normal = center * inverse
     normed[...] = normal
     inv_std[...] = inverse
-    half_a = width // HALVES
     scaled_rows = (normal * gain).astype(BF16)
     for h in range(HALVES):
-        rows_a[h, p] = scaled_rows[:, h * half_a : (h + 1) * half_a]
+        rows_a[h, p] = scaled_rows[:, h * half_width : (h + 1) * half_width]
 
     def forward_chunk(j, scaled):
         cols = slice(j * chunk, (j + 1) * chunk)
         hidden = jnp.dot(scaled, win[:, cols], preferred_element_type=F32)
         cdf = 0.5 * (1.0 + lax.erf(hidden * SQRT_HALF))
-        activated = (hidden * cdf).astype(BF16)
+        acted[:, cols] = (hidden * cdf).astype(BF16)
         slope[:, cols] = cdf + hidden * INV_ROOT_TAU * jnp.exp(-0.5 * hidden * hidden)
-        part = jnp.dot(activated, wout[cols, :], preferred_element_type=F32)
-        if j:
-            accum[...] += part
-        else:
-            accum[...] = part
 
     @pl.when(sec == 0)
     def _():
         scaled = jnp.concatenate([rows_a[h, p] for h in range(HALVES)], axis=1)
         for j in range(chunks):
             load_in[j].wait()
-            load_out[j].wait()
             forward_chunk(j, scaled)
+        for copy in load_out:
+            copy.wait()
 
     @pl.when(sec > 0)
     def _():
@@ -335,10 +363,13 @@
 
     @pl.when(sec < sections - 1)
     def _():
-        for m in range(batches):
-            part = slice(m * rows, (m + 1) * rows)
-            y_out[m] = (x_in[m].astype(F32) + scales * accum[part, :]).astype(BF16)
-            forward_copies[m].start()
+        values = acted[...]
+        for h in range(HALVES):
+            cols = slice(h * half_width, (h + 1) * half_width)
+            part = jnp.dot(values, wout[:, cols], preferred_element_type=F32)
+            output = x_in[h].reshape(tokens, half_width).astype(F32) + scales[:, cols] * part
+            y_out[h] = output.astype(BF16).reshape(batches, rows, half_width)
+            forward_copies[h].start()
 
     for h in range(HALVES):
         start_half(fa, h)
@@ -359,49 +390,42 @@
 
     @pl.when(sec == sections - 1)
     def _():
-        load_top.wait()
-
-    def backward_chunk(j, gz, onward):
+        for copy in load_top:
+            copy.wait()
+
+    cotangent = joined(g_in).astype(F32)
+    gz = (cotangent * scales).astype(BF16)
+    per = chunks // HALVES
+    for j in range(chunks):
         cols = slice(j * chunk, (j + 1) * chunk)
         grad_act = lax.dot_general(gz, wout[cols, :], NT, preferred_element_type=F32)
-        grad_hidden = (grad_act * slope[:, cols]).astype(BF16)
-        per = chunks // HALVES
         h, inner = j // per, j % per
-        rows_g[h, p, :, inner * chunk : (inner + 1) * chunk] = grad_hidden
-        if onward:
-            part = lax.dot_general(grad_hidden, win[:, cols], NT, preferred_element_type=F32)
-            if j:
-                accum[...] += part
-            else:
-                accum[...] = part
+        rows_g[h, p, :, inner * chunk : (inner + 1) * chunk] = (grad_act * slope[:, cols]).astype(BF16)
         if inner == per - 1:
             start_half(fg, h)
 
-    @pl.when(sec == 0)
-    def _():
-        gz = (g_in[...].reshape(tokens, width).astype(F32) * scales).astype(BF16)
-        for j in range(chunks):
-            backward_chunk(j, gz, False)
-
     @pl.when(sec > 0)
     def _():
-        gz = (g_in[...].reshape(tokens, width).astype(F32) * scales).astype(BF16)
-        for j in range(chunks):
-            backward_chunk(j, gz, True)
-        for m in range(batches):
-            part = slice(m * rows, (m + 1) * rows)
-            normal_part = normed[part, :]
-            grad_normed = accum[part, :] * gain
-            mean_one = jnp.mean(grad_normed, axis=-1, keepdims=True)
-            mean_two = jnp.mean(grad_normed * normal_part, axis=-1, keepdims=True)
-            grad_input = g_in[m].astype(F32) + inv_std[part, :] * (
-                grad_normed - mean_one - normal_part * mean_two
+        grad_hidden = jnp.concatenate([rows_g[h, p] for h in range(HALVES)], axis=1)
+        for h in range(HALVES):
+            cols = slice(h * half_width, (h + 1) * half_width)
+            accum[:, cols] = lax.dot_general(
+                grad_hidden, win[cols, :], NT, preferred_element_type=F32
             )
-            g_out[m] = grad_input.astype(BF16)
-            backward_copies[m].start()
+        normal = normed[...]
+        grad_normed = accum[...] * gain
+        mean_one = jnp.mean(grad_normed, axis=-1, keepdims=True)
+        mean_two = jnp.mean(grad_normed * normal, axis=-1, keepdims=True)
+        scale_back = inv_std[...]
+        for h in range(HALVES):
+            cols = slice(h * half_width, (h + 1) * half_width)
+            grad_input = g_in[h].reshape(tokens, half_width).astype(F32) + scale_back * (
+                accum[:, cols] * gain[:, cols] - mean_one - normed[:, cols] * mean_two
+            )
+            g_out[h] = grad_input.astype(BF16).reshape(batches, rows, half_width)
+            backward_copies[h].start()
 
     finish_gather(fg)
-    choose(fg)
     far_part(fg, 0)
     near_part(fg, 0, 0)
     near_part(fg, 0, 1)
@@ -444,6 +468,11 @@
                     f.near_copy[g][d][h].wait_send()
             for copy in f.z_copy[g]:
                 copy.wait_send()
+
+
+def scale_kernel(factor, act_ref, grad_ref, act_out, grad_out):
+    act_out[0] = act_ref[...] * factor
+    grad_out[0] = grad_ref[...] * factor
 
 
 def body(dp_count, sections, inputs, ln_gain, w_in, w_out, layer_scale, out_grad, owner_table):
@@ -487,24 +516,25 @@
         scratch_shapes=[
             pltpu.VMEM((width, hidden_width), BF16),
             pltpu.VMEM((hidden_width, width), BF16),
-            pltpu.VMEM((batches, rows, width), BF16),
-            pltpu.VMEM((batches, rows, width), BF16),
-            pltpu.VMEM((batches, rows, width), BF16),
-            pltpu.VMEM((batches, rows, width), BF16),
+            pltpu.VMEM((HALVES, batches, rows, width // HALVES), BF16),
+            pltpu.VMEM((HALVES, batches, rows, width // HALVES), BF16),
+            pltpu.VMEM((HALVES, batches, rows, width // HALVES), BF16),
+            pltpu.VMEM((HALVES, batches, rows, width // HALVES), BF16),
             pltpu.VMEM((tokens, width), F32),
             pltpu.VMEM((tokens, 1), F32),
             pltpu.VMEM((tokens, hidden_width), F32),
             pltpu.VMEM((tokens, width), F32),
+            pltpu.VMEM((tokens, hidden_width), BF16),
         ]
         + factor_scratch(block_a, width, 1)
         + factor_scratch(block_g, hidden_width, 2)
         + [
             dma((2, hidden_width // chunk)),
-            dma((2,)),
-            dma((2 * batches,)),
-            dma((2 * batches,)),
-            dma((2, 6)),
-            dma((2, 6)),
+            dma((2, HALVES * batches)),
+            dma((2 * HALVES,)),
+            dma((2 * HALVES,)),
+            dma((2, 8)),
+            dma((2, 8)),
             dma((2, 2, 6)),
             dma((2, 2, 6)),
             dma((2, 2, max(planes - 1, 1))),
@@ -515,7 +545,18 @@
         ),
         name="window",
     )(owner_table, inputs, out_grad, ln_gain, layer_scale, w_in[0], w_out[0])
-    return (act[None], grad[None])
+    factor = 1.0 / (tokens * dp_count)
+    return pl.pallas_call(
+        functools.partial(scale_kernel, factor),
+        out_shape=(
+            jax.ShapeDtypeStruct((1, block_a, width), F32),
+            jax.ShapeDtypeStruct((1, block_g, hidden_width), F32),
+        ),
+        in_specs=[vmem, vmem],
+        out_specs=(vmem, vmem),
+        compiler_params=pltpu.CompilerParams(vmem_limit_bytes=60 * 1024 * 1024),
+        name="mean",
+    )(act, grad)
 
 
 def solution(mesh):

time: 86 us -> 82.9 us (0.964)
  local copies, waits for them, and re-layouts: 3.14 us -> 0 us
    unnamed x2 -> x0, local copies, waits for them, and re-layouts: 3.14 us -> none
    pallas_call x1, Pallas kernels: 82 us -> 79.9 us  [body(): pl.pallas_call(functools.partial(kernel, dp_count, sections), out_shape=(...]
    pallas_call x0 -> x1, Pallas kernels: none -> 1.74 us  [body(): pl.pallas_call(functools.partial(scale_kernel, factor), out_shape=(jax.Sh...]
where the time goes in v3:
time: 82.9 us; the launch traced here: 82.2 us
  Pallas kernels  81.6 us (98%)
    pallas_call x1, Pallas kernels, body(): pl.pallas_call(functools.partial(kernel, dp_count, sections), out_shape=(...  79.9 us
    pallas_call x1, Pallas kernels, body(): pl.pallas_call(functools.partial(scale_kernel, factor), out_shape=(jax.Sh...  1.74 us

profile of v3, /device:TPU:8, one launch (start us, length us, event | category | flops | bytes accessed | tf_op | source)
XLA Modules:
  0.0 82.2 jit_solution(2733519853305967962)
XLA Ops:
  0.6 79.9 %window.1 = (f32[16,1024]{1,0:T(8,128)}, f32[32,2048]{1,0:T(8,128)}) custom-call(s32[64]{0:T(128)} %owner_ref.1, bf16[2,64,1024]{2,1,0:T(8,128)(2,1)} %x_hbm.1, bf16[2,64,1024]{2,1,0:T(8,128)(2,1)} %top_hbm.1, f32[1,1024]{1,0:T(1,128)} %gain_ref.1, f32[1,1024]{1,0:T(1,128)} %scale_ref.1, bf16[1024,2048]{1,0:T(8,128)(2,1)} %bitcast.2, bf16[2048,1024]{1,0:T(8,128)(2,1)} %bitcast.3), custom_call_target="tpu_custom_call" | custom-call | tf_op jit(solution)/shard_map/window/pallas_call | solution.py:508
  80.5 1.7 %mean.1 = (f32[1,16,1024]{2,1,0:T(8,128)}, f32[1,32,2048]{2,1,0:T(8,128)}) custom-call(f32[16,1024]{1,0:T(8,128)} %get-tuple-element.4.act_ref, f32[32,2048]{1,0:T(8,128)} %get-tuple-element.5.grad_ref), custom_call_target="tpu_custom_call" | custom-call | tf_op jit(solution)/shard_map/mean/pallas_call | solution.py:549

commit v4 on v3

--- a/solution.py
+++ b/solution.py
@@ -41,11 +41,13 @@
     slope,
     accum,
     acted,
+    win_t,
+    wout_t,
     *rest,
 ):
     (pick_a, rows_a, left_a, far_a, near_a, hold_a, sum_a, far_in_a, near_in_a, zs_a, zr_a) = rest[:11]
     (pick_g, rows_g, left_g, far_g, near_g, hold_g, sum_g, far_in_g, near_in_g, zs_g, zr_g) = rest[11:22]
-    (w_sem, io_sem, relay_s, relay_r, gat_s, gat_r, sca_s, sca_r, z_s, z_r) = rest[22:]
+    (w_sem, io_sem, relay_s, relay_r, gat_s, gat_r, sca_s, sca_r, z_s, z_r, turn) = rest[22:]
     planes = dp_count // (RING * RING)
     sec = lax.axis_index("section")
     me = lax.axis_index("dp")
@@ -232,6 +234,16 @@
                 :, i * tokens : (i + 1) * tokens
             ].astype(BF16)
 
+    def give_turn():
+        @pl.when(even)
+        def _():
+            pl.semaphore_signal(turn, inc=1, device_id=(me, lax.rem(sec + 1, sections)), device_id_type=MESH)
+
+    def take_turn():
+        @pl.when(jnp.logical_not(even))
+        def _():
+            pl.semaphore_wait(turn, 1)
+
     def finish_gather(f):
         choose(f, [p])
         f.plus[0].wait_recv()
@@ -242,6 +254,8 @@
         f.minus[4].start()
         f.plus[1].wait_recv()
         f.minus[0].wait_recv()
+        if f is fg:
+            give_turn()
         choose(f, [ring(p, -1), ring(p, 1)])
         f.plus[2].wait_recv()
         f.minus[3].wait_recv()
@@ -308,6 +322,17 @@
         own_part(fa, 0)
         relay_part(fa, 0)
 
+    def transpose_weights():
+        for source, target in ((wout, wout_t), (win, win_t)):
+            count = source.shape[0] // chunk
+
+            def step(i, carry):
+                at = pl.ds(pl.multiple_of(i * chunk, chunk), chunk)
+                target[:, at] = source[at, :].T
+                return carry
+
+            lax.fori_loop(0, count, step, 0)
+
     gain = gain_ref[...]
     scales = scale_ref[...]
 
@@ -316,6 +341,11 @@
         build_picks()
         for copy in load_in + load_out:
             copy.wait()
+
+        @pl.when(sec == sections - 1)
+        def _():
+            transpose_weights()
+
         for copy in forward_copies:
             copy.wait_recv()
 
@@ -378,6 +408,10 @@
     def _():
         build_picks()
 
+    @pl.when(sec < sections - 1)
+    def _():
+        transpose_weights()
+
     @pl.when(sec < sections // 2)
     def _():
         act_products()
@@ -398,7 +432,7 @@
     per = chunks // HALVES
     for j in range(chunks):
         cols = slice(j * chunk, (j + 1) * chunk)
-        grad_act = lax.dot_general(gz, wout[cols, :], NT, preferred_element_type=F32)
+        grad_act = jnp.dot(gz, wout_t[:, cols], preferred_element_type=F32)
         h, inner = j // per, j % per
         rows_g[h, p, :, inner * chunk : (inner + 1) * chunk] = (grad_act * slope[:, cols]).astype(BF16)
         if inner == per - 1:
@@ -409,9 +443,7 @@
         grad_hidden = jnp.concatenate([rows_g[h, p] for h in range(HALVES)], axis=1)
         for h in range(HALVES):
             cols = slice(h * half_width, (h + 1) * half_width)
-            accum[:, cols] = lax.dot_general(
-                grad_hidden, win[cols, :], NT, preferred_element_type=F32
-            )
+            accum[:, cols] = jnp.dot(grad_hidden, win_t[:, cols], preferred_element_type=F32)
         normal = normed[...]
         grad_normed = accum[...] * gain
         mean_one = jnp.mean(grad_normed, axis=-1, keepdims=True)
@@ -426,6 +458,7 @@
             backward_copies[h].start()
 
     finish_gather(fg)
+    take_turn()
     far_part(fg, 0)
     near_part(fg, 0, 0)
     near_part(fg, 0, 1)
@@ -525,6 +558,8 @@
             pltpu.VMEM((tokens, hidden_width), F32),
             pltpu.VMEM((tokens, width), F32),
             pltpu.VMEM((tokens, hidden_width), BF16),
+            pltpu.VMEM((hidden_width, width), BF16),
+            pltpu.VMEM((width, hidden_width), BF16),
         ]
         + factor_scratch(block_a, width, 1)
         + factor_scratch(block_g, hidden_width, 2)
@@ -539,6 +574,7 @@
             dma((2, 2, 6)),
             dma((2, 2, max(planes - 1, 1))),
             dma((2, 2, max(planes - 1, 1))),
+            pltpu.SemaphoreType.REGULAR,
         ],
         compiler_params=pltpu.CompilerParams(
             collective_id=0, has_side_effects=True, vmem_limit_bytes=60 * 1024 * 1024

time: 82.9 us -> 77.3 us (0.932)
  Pallas kernels: 81.6 us -> 75.6 us
    pallas_call x1, Pallas kernels: 79.9 us -> 73.9 us  [body(): pl.pallas_call(functools.partial(kernel, dp_count, sections), out_shape=(...]
where the time goes in v4:
time: 77.3 us; the launch traced here: 76.2 us
  Pallas kernels  75.6 us (98%)
    pallas_call x1, Pallas kernels, body(): pl.pallas_call(functools.partial(kernel, dp_count, sections), out_shape=(...  73.9 us
    pallas_call x1, Pallas kernels, body(): pl.pallas_call(functools.partial(scale_kernel, factor), out_shape=(jax.Sh...  1.74 us

profile of v4, /device:TPU:8, one launch (start us, length us, event | category | flops | bytes accessed | tf_op | source)
XLA Modules:
  0.0 76.2 jit_solution(8765481681679410773)
XLA Ops:
  0.6 73.9 %window.1 = (f32[16,1024]{1,0:T(8,128)}, f32[32,2048]{1,0:T(8,128)}) custom-call(s32[64]{0:T(128)} %owner_ref.1, bf16[2,64,1024]{2,1,0:T(8,128)(2,1)} %x_hbm.1, bf16[2,64,1024]{2,1,0:T(8,128)(2,1)} %top_hbm.1, f32[1,1024]{1,0:T(1,128)} %gain_ref.1, f32[1,1024]{1,0:T(1,128)} %scale_ref.1, bf16[1024,2048]{1,0:T(8,128)(2,1)} %bitcast.2, bf16[2048,1024]{1,0:T(8,128)(2,1)} %bitcast.3), custom_call_target="tpu_custom_call" | custom-call | tf_op jit(solution)/shard_map/window/pallas_call | solution.py:541
  74.5 1.7 %mean.1 = (f32[1,16,1024]{2,1,0:T(8,128)}, f32[1,32,2048]{2,1,0:T(8,128)}) custom-call(f32[16,1024]{1,0:T(8,128)} %get-tuple-element.4.act_ref, f32[32,2048]{1,0:T(8,128)} %get-tuple-element.5.grad_ref), custom_call_target="tpu_custom_call" | custom-call | tf_op jit(solution)/shard_map/mean/pallas_call | solution.py:585

commit v5 on v4

--- a/solution.py
+++ b/solution.py
@@ -114,7 +114,9 @@
         for copy in load_x:
             copy.start()
 
-    for copy in load_in + load_out:
+    for copy in load_in:
+        copy.start()
+    for copy in load_out:
         copy.start()
 
     @pl.when(sec == sections - 1)
@@ -376,18 +378,17 @@
 
     @pl.when(sec == 0)
     def _():
-        scaled = jnp.concatenate([rows_a[h, p] for h in range(HALVES)], axis=1)
-        for j in range(chunks):
-            load_in[j].wait()
-            forward_chunk(j, scaled)
+        for copy in load_in:
+            copy.wait()
+
+    scaled = jnp.concatenate([rows_a[h, p] for h in range(HALVES)], axis=1)
+    for j in range(chunks):
+        forward_chunk(j, scaled)
+
+    @pl.when(sec == 0)
+    def _():
         for copy in load_out:
             copy.wait()
-
-    @pl.when(sec > 0)
-    def _():
-        scaled = jnp.concatenate([rows_a[h, p] for h in range(HALVES)], axis=1)
-        for j in range(chunks):
-            forward_chunk(j, scaled)
 
     pl.semaphore_wait(barrier, len(greeted))
 
@@ -441,18 +442,22 @@
     @pl.when(sec > 0)
     def _():
         grad_hidden = jnp.concatenate([rows_g[h, p] for h in range(HALVES)], axis=1)
-        for h in range(HALVES):
-            cols = slice(h * half_width, (h + 1) * half_width)
-            accum[:, cols] = jnp.dot(grad_hidden, win_t[:, cols], preferred_element_type=F32)
-        normal = normed[...]
-        grad_normed = accum[...] * gain
-        mean_one = jnp.mean(grad_normed, axis=-1, keepdims=True)
-        mean_two = jnp.mean(grad_normed * normal, axis=-1, keepdims=True)
+        sum_one = sum_two = None
+        for n in range(width // chunk):
+            cols = slice(n * chunk, (n + 1) * chunk)
+            piece = jnp.dot(grad_hidden, win_t[:, cols], preferred_element_type=F32) * gain[:, cols]
+            accum[:, cols] = piece
+            one = jnp.sum(piece, axis=-1, keepdims=True)
+            two = jnp.sum(piece * normed[:, cols], axis=-1, keepdims=True)
+            sum_one = one if n == 0 else sum_one + one
+            sum_two = two if n == 0 else sum_two + two
+        mean_one = sum_one / width
+        mean_two = sum_two / width
         scale_back = inv_std[...]
         for h in range(HALVES):
             cols = slice(h * half_width, (h + 1) * half_width)
             grad_input = g_in[h].reshape(tokens, half_width).astype(F32) + scale_back * (
-                accum[:, cols] * gain[:, cols] - mean_one - normed[:, cols] * mean_two
+                accum[:, cols] - mean_one - normed[:, cols] * mean_two
             )
             g_out[h] = grad_input.astype(BF16).reshape(batches, rows, half_width)
             backward_copies[h].start()

time: 77.3 us -> 75.8 us (0.981)
  Pallas kernels: 75.6 us -> 74.6 us
    pallas_call x1, Pallas kernels: 73.9 us -> 72.9 us  [body(): pl.pallas_call(functools.partial(kernel, dp_count, sections), out_shape=(...]
where the time goes in v5:
time: 75.8 us; the launch traced here: 75.2 us
  Pallas kernels  74.6 us (98%)
    pallas_call x1, Pallas kernels, body(): pl.pallas_call(functools.partial(kernel, dp_count, sections), out_shape=(...  72.9 us
    pallas_call x1, Pallas kernels, body(): pl.pallas_call(functools.partial(scale_kernel, factor), out_shape=(jax.Sh...  1.74 us

profile of v5, /device:TPU:8, one launch (start us, length us, event | category | flops | bytes accessed | tf_op | source)
XLA Modules:
  0.0 75.2 jit_solution(9604754523218789270)
XLA Ops:
  0.6 72.9 %window.1 = (f32[16,1024]{1,0:T(8,128)}, f32[32,2048]{1,0:T(8,128)}) custom-call(s32[64]{0:T(128)} %owner_ref.1, bf16[2,64,1024]{2,1,0:T(8,128)(2,1)} %x_hbm.1, bf16[2,64,1024]{2,1,0:T(8,128)(2,1)} %top_hbm.1, f32[1,1024]{1,0:T(1,128)} %gain_ref.1, f32[1,1024]{1,0:T(1,128)} %scale_ref.1, bf16[1024,2048]{1,0:T(8,128)(2,1)} %bitcast.2, bf16[2048,1024]{1,0:T(8,128)(2,1)} %bitcast.3), custom_call_target="tpu_custom_call" | custom-call | tf_op jit(solution)/shard_map/window/pallas_call | solution.py:546
  73.5 1.7 %mean.1 = (f32[1,16,1024]{2,1,0:T(8,128)}, f32[1,32,2048]{2,1,0:T(8,128)}) custom-call(f32[16,1024]{1,0:T(8,128)} %get-tuple-element.4.act_ref, f32[32,2048]{1,0:T(8,128)} %get-tuple-element.5.grad_ref), custom_call_target="tpu_custom_call" | custom-call | tf_op jit(solution)/shard_map/mean/pallas_call | solution.py:590

commit v6 on v5

--- a/solution.py
+++ b/solution.py
@@ -275,9 +275,14 @@
         return pieces[0] if len(pieces) == 1 else jnp.concatenate(pieces, axis=1)
 
     def far_part(f, g):
-        part = part_of(f, g, 2)
+        dest = ring(q, 2)
+        extent = f.rows.shape[3]
+        left = f.left[pl.ds(pl.multiple_of(dest * f.span, f.span), f.span), :]
         for d in range(2):
-            f.far[g, d] = part[:, d * f.half : (d + 1) * f.half].astype(BF16)
+            at = g * 2 * f.half + d * f.half
+            source = f.rows[at // extent, :, :, at % extent : at % extent + f.half]
+            part = jnp.dot(left, source.reshape(RING * tokens, f.half), preferred_element_type=F32)
+            f.far[g, d] = part.astype(BF16)
             f.far_copy[g][d].start()
 
     def near_part(f, g, d):

time: 75.8 us -> 75.6 us (level)
  no operation moved by 1% of the time
where the time goes in v6:
time: 75.6 us; the launch traced here: 75.2 us
  Pallas kernels  74.6 us (99%)
    pallas_call x1, Pallas kernels, body(): pl.pallas_call(functools.partial(kernel, dp_count, sections), out_shape=(...  72.8 us
    pallas_call x1, Pallas kernels, body(): pl.pallas_call(functools.partial(scale_kernel, factor), out_shape=(jax.Sh...  1.74 us

profile of v6, /device:TPU:8, one launch (start us, length us, event | category | flops | bytes accessed | tf_op | source)
XLA Modules:
  0.0 75.2 jit_solution(16115228165434568091)
XLA Ops:
  0.6 72.8 %window.1 = (f32[16,1024]{1,0:T(8,128)}, f32[32,2048]{1,0:T(8,128)}) custom-call(s32[64]{0:T(128)} %owner_ref.1, bf16[2,64,1024]{2,1,0:T(8,128)(2,1)} %x_hbm.1, bf16[2,64,1024]{2,1,0:T(8,128)(2,1)} %top_hbm.1, f32[1,1024]{1,0:T(1,128)} %gain_ref.1, f32[1,1024]{1,0:T(1,128)} %scale_ref.1, bf16[1024,2048]{1,0:T(8,128)(2,1)} %bitcast.2, bf16[2048,1024]{1,0:T(8,128)(2,1)} %bitcast.3), custom_call_target="tpu_custom_call" | custom-call | tf_op jit(solution)/shard_map/window/pallas_call | solution.py:551
  73.5 1.7 %mean.1 = (f32[1,16,1024]{2,1,0:T(8,128)}, f32[1,32,2048]{2,1,0:T(8,128)}) custom-call(f32[16,1024]{1,0:T(8,128)} %get-tuple-element.4.act_ref, f32[32,2048]{1,0:T(8,128)} %get-tuple-element.5.grad_ref), custom_call_target="tpu_custom_call" | custom-call | tf_op jit(solution)/shard_map/mean/pallas_call | solution.py:595
